TPU v7x, 32 devices: a whole 2x2x4 slice. The times are simulated.
32 devices in a mesh: wide: 8 (over z, x), narrow: 4 (over y, core).
Axes of the slice: x: 2, y: 2, z: 4, core: 2. Of those that a mesh axis runs over, the one named last changes fastest.
Arguments:
- tokens: bfloat16 [384, 2560], P(('wide', 'narrow')), may hold values from -6 to 6
- scores: float32 [384], P(('wide', 'narrow')), may hold values from 0.25 to 1
- expert_ids: int32 [384], P(('wide', 'narrow')), may hold values from 0 to 15, as said below
- gate_halves: bfloat16 [32, 2560, 2048], P(('wide', 'narrow')), may hold values from -0.125 to 0.125
- up_halves: bfloat16 [32, 2560, 2048], P(('wide', 'narrow')), may hold values from -0.125 to 0.125
- shared_gate: bfloat16 [2560, 4096], P(None, 'narrow'), may hold values from -0.125 to 0.125
- shared_up: bfloat16 [2560, 4096], P(None, 'narrow'), may hold values from -0.125 to 0.125
Outputs:
- routed_hidden: bfloat16 [384, 4096], P(('wide', 'narrow'))
- shared_hidden: bfloat16 [384, 4096], P('wide', 'narrow')
Inputs may be any that keep to these rules, and one draw needn't show every extreme that they name: `expert_ids`: within the 12 rows of each device no expert is named more than 2 times, and one expert, the same for every device, is named exactly 2 times in the rows of every device.
All inputs are finite; a program needn't handle non-finite values.
Results may differ from a plain program's by a relative error of at most 0.0058.
Values may be sent and summed in bfloat16 or wider, within the bound.
A program may use at most 128 MiB of HBM per device.

v0:
```python
import functools

import jax
import jax.numpy as jnp
from jax import lax
from jax.experimental import pallas as pl
from jax.experimental.pallas import tpu as pltpu
from jax.sharding import PartitionSpec as P

CAP = 2
CHUNKS = 2
UNROLL = True
TILE = 512
MESH = pl.DeviceIdType.MESH


def silu_mul(gate_val, up_val):
    return (gate_val / (1.0 + jnp.exp(-gate_val))) * up_val


def kernel(
    wide, narrow,
    tokens_ref, scores_ref, ids_ref, gate_ref, up_ref, sgate_ref, sup_ref,
    routed_ref, shared_ref,
    wg, wu, sg, su, tok_all, outgoing, incoming, rows_x, sending, returned, flat,
    weight_sem, tok_send, tok_recv, out_send, out_recv, pair_send, pair_recv, back_send, back_recv,
):
    devices = wide * narrow
    my_w = lax.axis_index("wide")
    my_n = lax.axis_index("narrow")
    me = my_w * narrow + my_n
    rows, width = tokens_ref.shape
    padded = tok_all.shape[0] // narrow
    half_units = gate_ref.shape[2]
    experts = devices // 2
    part = half_units // CHUNKS
    shared_units = sgate_ref.shape[1]

    def dev(p):
        return (lax.div(p, narrow), lax.rem(p, narrow))

    weight_copies = [
        pltpu.make_async_copy(sgate_ref, sg, weight_sem.at[0]),
        pltpu.make_async_copy(sup_ref, su, weight_sem.at[1]),
    ]
    for j in range(CHUNKS):
        cols = pl.ds(j * part, part)
        weight_copies.append(
            pltpu.make_async_copy(gate_ref.at[0, :, cols], wg.at[:, cols], weight_sem.at[2 + 2 * j])
        )
        weight_copies.append(
            pltpu.make_async_copy(up_ref.at[0, :, cols], wu.at[:, cols], weight_sem.at[3 + 2 * j])
        )
    for copy in weight_copies:
        copy.start()

    barrier = pltpu.get_barrier_semaphore()

    def greet(k, carry):
        pl.semaphore_signal(barrier, inc=1, device_id=dev(lax.rem(me + k, devices)), device_id_type=MESH)
        return carry

    lax.fori_loop(1, devices, greet, 0, unroll=UNROLL)

    tok = tokens_ref[...]
    ids_lane = ids_ref[...]
    r_sub = lax.broadcasted_iota(jnp.int32, (rows, rows), 0)
    r_lane = lax.broadcasted_iota(jnp.int32, (rows, rows), 1)
    eye = r_sub == r_lane
    scores_col = jnp.sum(jnp.where(eye, scores_ref[...], 0.0), axis=1, keepdims=True)
    idsf_lane = ids_lane.astype(jnp.float32)
    ids_col = jnp.sum(jnp.where(eye, idsf_lane, 0.0), axis=1, keepdims=True)
    same = ids_col == idsf_lane
    rank_lane = jnp.sum(jnp.where(same & (r_sub < r_lane), 1.0, 0.0), axis=0, keepdims=True)
    rank_col = jnp.sum(jnp.where(same & (r_lane < r_sub), 1.0, 0.0), axis=1, keepdims=True)
    slot_lane = (idsf_lane * CAP + rank_lane).astype(jnp.int32)
    slot_col = (ids_col * CAP + rank_col).astype(jnp.int32)
    cells = experts * CAP
    place = jnp.where(
        lax.broadcasted_iota(jnp.int32, (cells, rows), 0) == slot_lane, 1.0, 0.0
    ).astype(jnp.bfloat16)
    pick = jnp.where(
        lax.broadcasted_iota(jnp.int32, (rows, cells), 1) == slot_col, 1.0, 0.0
    ).astype(jnp.bfloat16)
    scaled = (tok.astype(jnp.float32) * scores_col).astype(jnp.bfloat16)
    placed = jnp.dot(place, scaled, preferred_element_type=jnp.float32).astype(jnp.bfloat16)
    for e in range(experts):
        outgoing[e] = placed[CAP * e : CAP * e + CAP, :]
    my_tok = pl.ds(pl.multiple_of(my_n * padded, padded), padded)
    if padded > rows:
        tok_all[my_tok, :] = jnp.concatenate(
            [tok, jnp.zeros((padded - rows, width), jnp.bfloat16)], axis=0
        )
    else:
        tok_all[my_tok, :] = tok

    pl.semaphore_wait(barrier, devices - 1)

    chips = devices // 2
    my_chip = me // 2
    my_core = me % 2
    partner = dev(my_chip * 2 + 1 - my_core)
    lanes = narrow // 2
    my_lane = my_n // 2
    pair_n = my_lane * 2 + 1 - my_core

    def out_copy(k):
        chip = lax.rem(my_chip + k, chips)
        return pltpu.make_async_remote_copy(
            src_ref=outgoing.at[chip], dst_ref=incoming.at[my_core, my_chip],
            send_sem=out_send, recv_sem=out_recv,
            device_id=dev(chip * 2 + my_core), device_id_type=MESH,
        )

    def start_out(k, carry):
        out_copy(k).start()
        return carry

    lax.fori_loop(1, chips, start_out, 0, unroll=UNROLL)
    incoming[my_core, my_chip] = outgoing[my_chip]

    def tok_slab(n):
        return tok_all.at[pl.ds(pl.multiple_of(n * padded, padded), padded), :]

    def tok_copy(k, n):
        to = ((my_lane + k) % lanes) * 2 + my_core
        return pltpu.make_async_remote_copy(
            src_ref=tok_slab(n), dst_ref=tok_slab(n),
            send_sem=tok_send.at[k], recv_sem=tok_recv.at[k],
            device_id=(my_w, to), device_id_type=MESH,
        )

    def tok_pass(k, n):
        return pltpu.make_async_remote_copy(
            src_ref=tok_slab(n), dst_ref=tok_slab(n),
            send_sem=tok_send.at[lanes + k], recv_sem=tok_recv.at[lanes + k],
            device_id=(my_w, pair_n), device_id_type=MESH,
        )

    for k in range(1, lanes):
        tok_copy(k, my_n).start()
    tok_pass(0, my_n).start()

    others = pl.ds(0, chips - 1)
    all_out = pltpu.make_async_remote_copy(
        src_ref=outgoing.at[others], dst_ref=incoming.at[my_core, others],
        send_sem=out_send, recv_sem=out_recv,
        device_id=partner, device_id_type=MESH,
    )
    all_out.wait_recv()

    def pair_copy(core):
        return pltpu.make_async_remote_copy(
            src_ref=incoming.at[core], dst_ref=incoming.at[core],
            send_sem=pair_send, recv_sem=pair_recv,
            device_id=partner, device_id_type=MESH,
        )

    pair_copy(my_core).start()
    for k in range(1, lanes):
        origin = ((my_lane + lanes - k) % lanes) * 2 + my_core
        tok_copy(k, origin).wait_recv()
        tok_pass(k, origin).start()

    def fill_rows(core):
        first = pl.multiple_of(core * (chips * CAP), chips * CAP)
        half = rows_x.at[pl.ds(first, chips * CAP), :]
        for s in range(chips):
            half[CAP * s : CAP * s + CAP, :] = incoming[core, s]

    fill_rows(my_core)
    pair_copy(1 - my_core).wait_recv()
    fill_rows(1 - my_core)

    my_slot = my_core * chips + my_chip

    def back_copy(j, k):
        p = lax.rem(me + k, devices)
        return pltpu.make_async_remote_copy(
            src_ref=sending.at[j, lax.rem(p, 2) * chips + lax.div(p, 2)],
            dst_ref=returned.at[j, my_slot],
            send_sem=back_send.at[j], recv_sem=back_recv.at[j],
            device_id=dev(p), device_id_type=MESH,
        )

    def all_back(j):
        rest = pl.ds(0, devices - 1)
        return pltpu.make_async_remote_copy(
            src_ref=sending.at[j, rest], dst_ref=returned.at[j, rest],
            send_sem=back_send.at[j], recv_sem=back_recv.at[j],
            device_id=partner, device_id_type=MESH,
        )

    step_cols = min(TILE, part)
    for j in range(CHUNKS):
        weight_copies[2 + 2 * j].wait()
        weight_copies[3 + 2 * j].wait()

        def routed_step(i, carry):
            at = pl.multiple_of(j * part + i * step_cols, step_cols)
            cols = pl.ds(at, step_cols)
            gate_val = jnp.dot(rows_x[...], wg[:, cols], preferred_element_type=jnp.float32)
            up_val = jnp.dot(rows_x[...], wu[:, cols], preferred_element_type=jnp.float32)
            hidden = silu_mul(gate_val, up_val).astype(jnp.bfloat16)
            local = pl.ds(pl.multiple_of(i * step_cols, step_cols), step_cols)
            for s in range(devices):
                at_row = CAP * s
                sending[j, s, :, local] = hidden[at_row : at_row + CAP, :]
            return carry

        lax.fori_loop(0, part // step_cols, routed_step, 0)

        def start_back(k, carry):
            back_copy(j, k).start()
            return carry

        lax.fori_loop(1, devices, start_back, 0, unroll=UNROLL)
        returned[j, my_slot] = sending[j, my_slot]

    for k in range(lanes):
        origin = ((my_lane + lanes - k) % lanes) * 2 + 1 - my_core
        tok_pass(k, origin).wait_recv()
    weight_copies[0].wait()
    weight_copies[1].wait()

    tile = min(TILE, shared_units)

    def shared_step(i, carry):
        cols = pl.ds(pl.multiple_of(i * tile, tile), tile)
        gate_val = jnp.dot(tok_all[...], sg[:, cols], preferred_element_type=jnp.float32)
        up_val = jnp.dot(tok_all[...], su[:, cols], preferred_element_type=jnp.float32)
        hidden = silu_mul(gate_val, up_val)
        packed = jnp.concatenate(
            [hidden[n * padded : n * padded + rows, :] for n in range(narrow)], axis=0
        )
        shared_ref[:, cols] = packed.astype(jnp.bfloat16)
        return carry

    lax.fori_loop(0, shared_units // tile, shared_step, 0)

    for j in range(CHUNKS):
        all_back(j).wait_recv()
        for h in range(2):
            for e in range(experts):
                flat[CAP * e : CAP * e + CAP, :] = returned[j, h * experts + e]
            got = jnp.dot(pick, flat[...], preferred_element_type=jnp.float32)
            start = h * half_units + j * part
            routed_ref[:, start : start + part] = got.astype(jnp.bfloat16)

    for k in range(1, lanes):
        tok_copy(k, my_n).wait_send()
    for k in range(lanes):
        tok_pass(k, my_n).wait_send()
    pair_copy(my_core).wait_send()

    all_out.wait_send()
    for j in range(CHUNKS):
        all_back(j).wait_send()


def hand_on(routed_in, shared_in, routed_out, shared_out):
    routed_out[...] = routed_in[...]
    shared_out[...] = shared_in[...]


def shards(wide, narrow, tokens, scores, expert_ids, gate_halves, up_halves, shared_gate, shared_up):
    devices = wide * narrow
    rows, width = tokens.shape
    half_units = gate_halves.shape[2]
    shared_units = shared_gate.shape[1]
    padded = -(-rows // 16) * 16
    part = half_units // CHUNKS
    bf16 = jnp.bfloat16
    vmem = pl.BlockSpec(memory_space=pltpu.VMEM)
    hbm = pl.BlockSpec(memory_space=pl.ANY)
    dma = pltpu.SemaphoreType.DMA
    outs = pl.pallas_call(
        functools.partial(kernel, wide, narrow),
        out_shape=(
            jax.ShapeDtypeStruct((rows, 2 * half_units), bf16),
            jax.ShapeDtypeStruct((rows * narrow, shared_units), bf16),
        ),
        in_specs=[vmem, vmem, vmem, hbm, hbm, hbm, hbm],
        out_specs=(vmem, vmem),
        scratch_shapes=[
            pltpu.VMEM((width, half_units), bf16),
            pltpu.VMEM((width, half_units), bf16),
            pltpu.VMEM((width, shared_units), bf16),
            pltpu.VMEM((width, shared_units), bf16),
            pltpu.VMEM((narrow * padded, width), bf16),
            pltpu.VMEM((devices // 2, CAP, width), bf16),
            pltpu.VMEM((2, devices // 2, CAP, width), bf16),
            pltpu.VMEM((devices * CAP, width), bf16),
            pltpu.VMEM((CHUNKS, devices, CAP, part), bf16),
            pltpu.VMEM((CHUNKS, devices, CAP, part), bf16),
            pltpu.VMEM((devices // 2 * CAP, part), bf16),
            dma((2 + 2 * CHUNKS,)),
            dma((narrow,)),
            dma((narrow,)),
            dma,
            dma,
            dma,
            dma,
            dma((CHUNKS,)),
            dma((CHUNKS,)),
        ],
        compiler_params=pltpu.CompilerParams(collective_id=0, has_side_effects=True, vmem_limit_bytes=60 * 1024 * 1024),
    )(tokens, scores[None, :], expert_ids[None, :], gate_halves, up_halves, shared_gate, shared_up)
    return pl.pallas_call(
        hand_on,
        out_shape=tuple(jax.ShapeDtypeStruct(o.shape, o.dtype) for o in outs),
        in_specs=[vmem, vmem],
        out_specs=(vmem, vmem),
    )(*outs)


def solution(mesh):
    placed = (
        P(("wide", "narrow"), None),
        P(("wide", "narrow")),
        P(("wide", "narrow")),
        P(("wide", "narrow"), None, None),
        P(("wide", "narrow"), None, None),
        P(None, "narrow"),
        P(None, "narrow"),
    )
    return jax.shard_map(
        functools.partial(shards, mesh.shape["wide"], mesh.shape["narrow"]),
        mesh=mesh,
        in_specs=placed,
        out_specs=(P(("wide", "narrow"), None), P("wide", "narrow")),
        check_vma=False,
    )
```

profile of v0, /device:TPU:0, one launch (start us, length us, event | category | flops | bytes accessed | tf_op | source)
XLA Modules:
  0.0 27.4 jit_solution(3096488650748678119)
XLA Ops:
  0.6 25.1 %shard_map.86 = (bf16[12,4096]{1,0:T(8,128)(2,1)}, bf16[48,1024]{1,0:T(8,128)(2,1)}) custom-call(bf16[12,2560]{1,0:T(8,128)(2,1)} %tokens_ref.1, f32[1,12]{1,0:T(1,128)} %bitcast.2, s32[1,12]{1,0:T(1,128)} %bitcast.3, bf16[1,2560,2048]{2,1,0:T(8,128)(2,1)} %gate_ref.1, bf16[1,2560,2048]{2,1,0:T(8,128)(2,1)} %up_ref.1, bf16[2560,1024]{1,0:T(8,128)(2,1)} %sgate_ref.1, ...), custom_call_target="tpu_custom_call" | custom-call | tf_op jit(solution)/shard_map/pallas_call | solution.py:277
  25.7 1.7 %shard_map.87 = (bf16[12,4096]{1,0:T(8,128)(2,1)}, bf16[48,1024]{1,0:T(8,128)(2,1)}) custom-call(bf16[12,4096]{1,0:T(8,128)(2,1)} %get-tuple-element.4.routed_in, bf16[48,1024]{1,0:T(8,128)(2,1)} %get-tuple-element.5.shared_in), custom_call_target="tpu_custom_call" | custom-call | tf_op jit(solution)/shard_map/pallas_call | solution.py:309
where the time goes:
time: 27.6 us; the launch traced here: 27.4 us
  Pallas kernels  26.7 us (97%)
  between operations  0.64 us (2%)
    pallas_call x1, Pallas kernels, shards(): pl.pallas_call(functools.partial(kernel, wide, narrow), out_shape=(jax.Sh...  25.1 us
    pallas_call x1, Pallas kernels, shards(): pl.pallas_call(hand_on, out_shape=tuple((jax.ShapeDtypeStruct(o.shape, o....  1.65 us

commit v1 on v0

--- a/solution.py
+++ b/solution.py
@@ -11,6 +11,7 @@
 CHUNKS = 2
 UNROLL = True
 TILE = 512
+LIMIT = 44 * 1024 * 1024
 MESH = pl.DeviceIdType.MESH
 
 
@@ -20,15 +21,22 @@
 
 def kernel(
     wide, narrow,
-    tokens_ref, scores_ref, ids_ref, gate_ref, up_ref, sgate_ref, sup_ref,
+    tokens_in, scores_in, ids_in, gate_ref, up_ref, sgate_ref, sup_ref,
     routed_ref, shared_ref,
-    wg, wu, sg, su, tok_all, outgoing, incoming, rows_x, sending, returned, flat,
-    weight_sem, tok_send, tok_recv, out_send, out_recv, pair_send, pair_recv, back_send, back_recv,
+    tokens_ref, scores_ref, ids_ref, wg, wu, sg, su, tok_all, outgoing, incoming, rows_x, sending, returned, flat,
+    input_sem, weight_sem, tok_send, tok_recv, out_send, out_recv, pair_send, pair_recv, back_send, back_recv,
 ):
     devices = wide * narrow
     my_w = lax.axis_index("wide")
     my_n = lax.axis_index("narrow")
     me = my_w * narrow + my_n
+    input_copies = [
+        pltpu.make_async_copy(tokens_in, tokens_ref, input_sem.at[0]),
+        pltpu.make_async_copy(scores_in, scores_ref, input_sem.at[1]),
+        pltpu.make_async_copy(ids_in, ids_ref, input_sem.at[2]),
+    ]
+    for copy in input_copies:
+        copy.start()
     rows, width = tokens_ref.shape
     padded = tok_all.shape[0] // narrow
     half_units = gate_ref.shape[2]
@@ -38,6 +46,14 @@
 
     def dev(p):
         return (lax.div(p, narrow), lax.rem(p, narrow))
+
+    barrier = pltpu.get_barrier_semaphore()
+
+    def greet(k, carry):
+        pl.semaphore_signal(barrier, inc=1, device_id=dev(lax.rem(me + k, devices)), device_id_type=MESH)
+        return carry
+
+    lax.fori_loop(1, devices, greet, 0, unroll=UNROLL)
 
     weight_copies = [
         pltpu.make_async_copy(sgate_ref, sg, weight_sem.at[0]),
@@ -54,14 +70,8 @@
     for copy in weight_copies:
         copy.start()
 
-    barrier = pltpu.get_barrier_semaphore()
-
-    def greet(k, carry):
-        pl.semaphore_signal(barrier, inc=1, device_id=dev(lax.rem(me + k, devices)), device_id_type=MESH)
-        return carry
-
-    lax.fori_loop(1, devices, greet, 0, unroll=UNROLL)
-
+    for copy in input_copies:
+        copy.wait()
     tok = tokens_ref[...]
     ids_lane = ids_ref[...]
     r_sub = lax.broadcasted_iota(jnp.int32, (rows, rows), 0)
@@ -258,9 +268,15 @@
         all_back(j).wait_send()
 
 
-def hand_on(routed_in, shared_in, routed_out, shared_out):
-    routed_out[...] = routed_in[...]
-    shared_out[...] = shared_in[...]
+def hand_on(routed_in, shared_in, routed_out, shared_out, sem):
+    copies = [
+        pltpu.make_async_copy(routed_in, routed_out, sem.at[0]),
+        pltpu.make_async_copy(shared_in, shared_out, sem.at[1]),
+    ]
+    for copy in copies:
+        copy.start()
+    for copy in copies:
+        copy.wait()
 
 
 def shards(wide, narrow, tokens, scores, expert_ids, gate_halves, up_halves, shared_gate, shared_up):
@@ -280,9 +296,12 @@
             jax.ShapeDtypeStruct((rows, 2 * half_units), bf16),
             jax.ShapeDtypeStruct((rows * narrow, shared_units), bf16),
         ),
-        in_specs=[vmem, vmem, vmem, hbm, hbm, hbm, hbm],
+        in_specs=[hbm] * 7,
         out_specs=(vmem, vmem),
         scratch_shapes=[
+            pltpu.VMEM((rows, width), bf16),
+            pltpu.VMEM((1, rows), jnp.float32),
+            pltpu.VMEM((1, rows), jnp.int32),
             pltpu.VMEM((width, half_units), bf16),
             pltpu.VMEM((width, half_units), bf16),
             pltpu.VMEM((width, shared_units), bf16),
@@ -294,6 +313,7 @@
             pltpu.VMEM((CHUNKS, devices, CAP, part), bf16),
             pltpu.VMEM((CHUNKS, devices, CAP, part), bf16),
             pltpu.VMEM((devices // 2 * CAP, part), bf16),
+            dma((3,)),
             dma((2 + 2 * CHUNKS,)),
             dma((narrow,)),
             dma((narrow,)),
@@ -304,13 +324,18 @@
             dma((CHUNKS,)),
             dma((CHUNKS,)),
         ],
-        compiler_params=pltpu.CompilerParams(collective_id=0, has_side_effects=True, vmem_limit_bytes=60 * 1024 * 1024),
-    )(tokens, scores[None, :], expert_ids[None, :], gate_halves, up_halves, shared_gate, shared_up)
+        compiler_params=pltpu.CompilerParams(collective_id=0, has_side_effects=True, vmem_limit_bytes=LIMIT),
+    )(*(
+        pltpu.with_memory_space_constraint(a, pltpu.HBM)
+        for a in (tokens, scores[None, :], expert_ids[None, :], gate_halves, up_halves, shared_gate, shared_up)
+    ))
     return pl.pallas_call(
         hand_on,
         out_shape=tuple(jax.ShapeDtypeStruct(o.shape, o.dtype) for o in outs),
         in_specs=[vmem, vmem],
-        out_specs=(vmem, vmem),
+        out_specs=(hbm, hbm),
+        scratch_shapes=[dma((2,))],
+        compiler_params=pltpu.CompilerParams(vmem_limit_bytes=1024 * 1024),
     )(*outs)
 
 

time: 27.6 us -> 25.1 us (0.909)
  Pallas kernels: 26.7 us -> 24.3 us
    pallas_call x1, Pallas kernels: 25.1 us -> 23.6 us  [shards(): pl.pallas_call(functools.partial(kernel, wide, narrow), out_shape=(jax.Sh...]
    pallas_call x1, Pallas kernels: 1.65 us -> 0.7 us  [shards(): pl.pallas_call(hand_on, out_shape=tuple((jax.ShapeDtypeStruct(o.shape, o....]
where the time goes in v1:
time: 25.1 us; the launch traced here: 25 us
  Pallas kernels  24.3 us (97%)
  between operations  0.64 us (3%)
    pallas_call x1, Pallas kernels, shards(): pl.pallas_call(functools.partial(kernel, wide, narrow), out_shape=(jax.Sh...  23.6 us
    pallas_call x1, Pallas kernels, shards(): pl.pallas_call(hand_on, out_shape=tuple((jax.ShapeDtypeStruct(o.shape, o....  0.7 us

profile of v1, /device:TPU:0, one launch (start us, length us, event | category | flops | bytes accessed | tf_op | source)
XLA Modules:
  0.0 25.0 jit_solution(13648926380776860346)
XLA Ops:
  0.6 23.6 %shard_map.86 = (bf16[12,4096]{1,0:T(8,128)(2,1)S(1)}, bf16[48,1024]{1,0:T(8,128)(2,1)S(1)}) custom-call(bf16[12,2560]{1,0:T(8,128)(2,1)} %tokens_in.1, f32[1,12]{1,0:T(1,128)} %bitcast.2, s32[1,12]{1,0:T(1,128)} %bitcast.3, bf16[1,2560,2048]{2,1,0:T(8,128)(2,1)} %gate_ref.1, bf16[1,2560,2048]{2,1,0:T(8,128)(2,1)} %up_ref.1, bf16[2560,1024]{1,0:T(8,128)(2,1)} %sgate_ref.1, ...), custom_call_target="tpu_custom_call" | custom-call | tf_op jit(solution)/shard_map/pallas_call | solution.py:293
  24.3 0.7 %shard_map.87 = (bf16[12,4096]{1,0:T(8,128)(2,1)}, bf16[48,1024]{1,0:T(8,128)(2,1)}) custom-call(bf16[12,4096]{1,0:T(8,128)(2,1)S(1)} %get-tuple-element.4.routed_in, bf16[48,1024]{1,0:T(8,128)(2,1)S(1)} %get-tuple-element.5.shared_in), custom_call_target="tpu_custom_call" | custom-call | tf_op jit(solution)/shard_map/pallas_call | solution.py:332
